TPU v7x, 128 devices: a whole 4x4x4 slice. The times are simulated.
128 devices in a mesh: section: 2 (over z_hi), seq: 8 (over x, z_lo), expert: 8 (over y, core).
Axes of the slice: x: 4, y: 4, z: 4 (z_hi: 2, z_lo: 2; z = z_hi * 2 + z_lo), core: 2. Of those that a mesh axis runs over, the one named last changes fastest.
Arguments:
- tokens: bfloat16 [2, 1024, 2048], P(None, ('seq', 'expert')), may hold values from -12 to 12
- prompt_lengths: int32 [2, 3], replicated, may hold values from 1 to 512, 1024 in all within a row
- cache_lengths: int32 [2, 3], replicated, may hold values from 1 to 1024, 2048 in all within a row
- kv_cache: bfloat16 [2, 2048, 2, 2048], P(None, 'seq', None, 'expert'), may hold values from -360 to 360
- attn_routes: int32 [2, 1024, 2], P(None, 'seq'), may hold values from 0 to 3, all different within a row
- ffn_routes: int32 [2, 1024, 2], P(None, ('seq', 'expert')), may hold values from 0 to 7, all different within a row; in each aligned block of 16 rows (0 to 15, 16 to 31, ..., all dimensions but the last counted through in order) at most 8 rows name the same one
- attn_gain: float32 [2048], replicated, may hold values from 0.1 to 1.9
- ffn_gain: float32 [2048], replicated, may hold values from 0.1 to 1.9
- attn_mix: bfloat16 [2048, 4], replicated, may hold values from -0.125 to 0.125
- query_weight: bfloat16 [2048, 4, 2048], P(None, None, 'expert'), may hold values from -0.125 to 0.125
- kv_weight: bfloat16 [2048, 2, 2048], P(None, None, 'expert'), may hold values from -0.125 to 0.125
- out_weight: bfloat16 [4, 2048, 2048], P(None, 'expert'), may hold values from -0.125 to 0.125
- ffn_mix: bfloat16 [2048, 8], replicated, may hold values from -0.125 to 0.125
- in_weight: bfloat16 [8, 2048, 2, 5632], P('expert', None, None, 'seq'), may hold values from -0.125 to 0.125
- down_weight: bfloat16 [8, 5632, 2048], P('expert', 'seq'), may hold values from -0.078125 to 0.078125
Outputs:
- layer_out: bfloat16 [2, 1024, 2048], P('section', ('seq', 'expert'))
Inputs may be any that keep to these rules, and one draw needn't show every extreme that they name: `prompt_lengths`: each row sums to 1024; its largest entry is 512. `cache_lengths`: each row sums to 2048; its largest entry is 1024. `attn_routes`: the two experts of a position differ; every expert is named somewhere. `ffn_routes`: the two experts of a position differ. Taking all micro-batches and positions in order, in each aligned block of 16 positions (the rows of one device) no expert is named more than 8 times, and some block names one exactly 8 times.
All inputs are finite; a program needn't handle non-finite values.
Results may differ from a plain program's by a relative error of at most 0.029.
Values may be sent and summed in bfloat16 or wider, within the bound.
A program may use at most 128 MiB of HBM per device.

v0:
```python
import jax
import jax.numpy as jnp
from jax import lax
from jax.sharding import PartitionSpec as P

HEAD_DIM = 128
EPS = 1e-06
THETA = 10000.0
NEGATIVE = -1e30


def rms_scale(values, gain):
    widened = values.astype(jnp.float32)
    inverse = lax.rsqrt(jnp.mean(widened * widened, axis=-1, keepdims=True) + EPS)
    return (widened * inverse * gain).astype(jnp.bfloat16)


def segment_of(row_index, lengths):
    ends = jnp.cumsum(lengths)
    return jnp.sum((row_index[:, None] >= ends[None, :]).astype(jnp.int32), axis=1)


def positions(row_index, lengths, cached):
    ends = jnp.cumsum(lengths)
    segment = jnp.sum((row_index[:, None] >= ends[None, :]).astype(jnp.int32), axis=1)
    matched = segment[:, None] == jnp.arange(lengths.shape[0], dtype=jnp.int32)[None, :]
    begins = jnp.sum(jnp.where(matched, (ends - lengths)[None, :], 0), axis=1)
    offsets = jnp.sum(jnp.where(matched, cached[None, :], 0), axis=1)
    return (segment, offsets + row_index - begins)


def rotate(values, place):
    half_dim = values.shape[-1] // 2
    freq = THETA ** (-jnp.arange(half_dim, dtype=jnp.float32) / half_dim)
    angle = place.astype(jnp.float32)[:, None] * freq[None, :]
    shape = (values.shape[0],) + (1,) * (values.ndim - 2) + (half_dim,)
    cosine = jnp.cos(angle).reshape(shape)
    sine = jnp.sin(angle).reshape(shape)
    former = values[..., :half_dim]
    latter = values[..., half_dim:]
    return jnp.concatenate(
        [former * cosine - latter * sine, latter * cosine + former * sine], axis=-1
    )


def route_gates(normed, mixing, routes):
    logits = jnp.dot(normed, mixing, preferred_element_type=jnp.float32)
    chosen = jnp.take_along_axis(logits, routes, axis=1)
    leading = jax.nn.sigmoid(chosen[:, 0] - chosen[:, 1])
    return jnp.stack([leading, 1.0 - leading], axis=1)


def select_batch(values, batch):
    return lax.dynamic_index_in_dim(values, batch, 0, keepdims=False)


def attention_block(
    own_rows, lengths, cached, cache_rows, routes, gain, mixing, query_weight, kv_weight, out_weight
):
    gathered = lax.all_gather(own_rows, "expert", axis=0, tiled=True)
    count = gathered.shape[0]
    normed = rms_scale(gathered, gain)
    row_index = lax.axis_index("seq") * count + jnp.arange(count, dtype=jnp.int32)
    segment, place = positions(row_index, lengths, cached)
    gates = route_gates(normed, mixing, routes)
    experts = query_weight.shape[1]
    width = query_weight.shape[2]
    local_heads = width // HEAD_DIM
    query_all = jnp.dot(
        normed, query_weight.reshape(query_weight.shape[0], -1), preferred_element_type=jnp.float32
    )
    query_all = query_all.reshape(count, experts, local_heads, HEAD_DIM)
    query = jnp.take_along_axis(query_all, routes[:, :, None, None], axis=1)
    query = rotate(query, place).astype(jnp.bfloat16)
    queries = query.reshape(count * 2, local_heads, HEAD_DIM)
    projected = jnp.dot(
        normed, kv_weight.reshape(kv_weight.shape[0], -1), preferred_element_type=jnp.float32
    )
    projected = projected.reshape(count, 2, local_heads, HEAD_DIM)
    fresh_keys = rotate(projected[:, 0], place).astype(jnp.bfloat16).reshape(count, width)
    fresh_values = projected[:, 1].astype(jnp.bfloat16).reshape(count, width)
    fresh = jnp.stack([fresh_keys, fresh_values], axis=1)
    query_segment = jnp.repeat(segment, 2)
    query_index = jnp.repeat(row_index, 2)
    scale = HEAD_DIM ** (-0.5)
    slots = count * 2

    def absorb(carried, piece, allowed):
        row_top, row_total, row_sum = carried
        keys = piece[:, 0].reshape(-1, local_heads, HEAD_DIM)
        values = piece[:, 1].reshape(-1, local_heads, HEAD_DIM)
        scores = (
            jnp.einsum("qhd,khd->hqk", queries, keys, preferred_element_type=jnp.float32) * scale
        )
        scores = jnp.where(allowed[None], scores, NEGATIVE)
        new_top = jnp.maximum(row_top, jnp.max(scores, axis=2))
        weights = jnp.where(allowed[None], jnp.exp(scores - new_top[:, :, None]), 0.0)
        shrink = jnp.exp(row_top - new_top)
        row_total = row_total * shrink + jnp.sum(weights, axis=2)
        row_sum = row_sum * shrink[:, :, None] + jnp.einsum(
            "hqk,khd->hqd", weights.astype(jnp.bfloat16), values, preferred_element_type=jnp.float32
        )
        return (new_top, row_total, row_sum)

    initial = (
        jnp.full((local_heads, slots), NEGATIVE, jnp.float32),
        jnp.zeros((local_heads, slots), jnp.float32),
        jnp.zeros((local_heads, slots, HEAD_DIM), jnp.float32),
    )
    piece = lax.all_gather(cache_rows, "seq", axis=0, tiled=True)
    key_segment = segment_of(jnp.arange(piece.shape[0], dtype=jnp.int32), cached)
    allowed = query_segment[:, None] == key_segment[None, :]
    carried = absorb(initial, piece, allowed)
    piece = lax.all_gather(fresh, "seq", axis=0, tiled=True)
    key_index = jnp.arange(piece.shape[0], dtype=jnp.int32)
    key_segment = segment_of(key_index, lengths)
    allowed = (query_segment[:, None] == key_segment[None, :]) & (
        key_index[None, :] <= query_index[:, None]
    )
    row_top, row_total, row_sum = absorb(carried, piece, allowed)
    attended = (row_sum / row_total[:, :, None]).astype(jnp.bfloat16)
    attended = attended.transpose(1, 0, 2).reshape(count, 2, width)
    select = (routes[:, :, None] == jnp.arange(experts, dtype=jnp.int32)[None, None, :]).astype(
        jnp.float32
    )
    select = select * gates[:, :, None]
    spread = jnp.einsum("tka,tkd->tad", select, attended.astype(jnp.float32)).astype(jnp.bfloat16)
    spread = spread.reshape(count, experts * width)
    out_flat = out_weight.reshape(experts * width, -1)
    term = lax.psum_scatter(
        jnp.dot(spread, out_flat, preferred_element_type=jnp.float32).astype(jnp.bfloat16),
        "expert",
        scatter_dimension=0,
        tiled=True,
    ).astype(jnp.float32)
    return (own_rows.astype(jnp.float32) + term).astype(jnp.bfloat16)


def expert_hidden(rows, in_weight):
    single = in_weight[0]
    both = jnp.dot(rows, single.reshape(single.shape[0], -1), preferred_element_type=jnp.float32)
    both = both.reshape(rows.shape[0], 2, -1)
    return (jax.nn.silu(both[:, 0]) * both[:, 1]).astype(jnp.bfloat16)


def expert_block(middle, routes, gain, mixing, in_weight, down_weight):
    rows = middle.shape[0]
    features = middle.shape[1]
    normed = rms_scale(middle, gain)
    gates = route_gates(normed, mixing, routes)
    experts = mixing.shape[1]
    capacity = max(2, 4 * rows // experts)
    flat = routes.reshape(-1)
    member = (flat[:, None] == jnp.arange(experts, dtype=jnp.int32)[None, :]).astype(jnp.int32)
    earlier = jnp.cumsum(member, axis=0) - member
    slot = jnp.sum(earlier * member, axis=1)
    target = flat * capacity + slot
    table = (jnp.arange(experts * capacity, dtype=jnp.int32)[:, None] == target[None, :]).astype(
        jnp.bfloat16
    )
    table = jnp.sum(table.reshape(experts * capacity, rows, 2), axis=2)
    buffer = jnp.dot(table, normed, preferred_element_type=jnp.float32).astype(jnp.bfloat16)
    buffer = buffer.reshape(experts, capacity, features)
    seq_count = lax.axis_size("seq")
    copies = jnp.broadcast_to(buffer[None], (seq_count,) + buffer.shape)
    copies = copies.reshape(seq_count * experts, capacity, features)
    arrived = lax.all_to_all(copies, ("seq", "expert"), split_axis=0, concat_axis=0, tiled=True)
    flat_rows = arrived.reshape(-1, features)
    hidden = expert_hidden(flat_rows, in_weight)
    partial_value = jnp.dot(hidden, down_weight[0], preferred_element_type=jnp.float32)
    partial_value = partial_value.astype(jnp.bfloat16).reshape(arrived.shape)
    returned = lax.all_to_all(
        partial_value, ("seq", "expert"), split_axis=0, concat_axis=0, tiled=True
    )
    results = jnp.sum(
        returned.reshape(seq_count, experts, capacity, features).astype(jnp.float32), axis=0
    )
    picked = jnp.take(results.reshape(experts * capacity, features), target, axis=0).reshape(
        rows, 2, features
    )
    mixture = gates[:, 0:1] * picked[:, 0] + gates[:, 1:2] * picked[:, 1]
    return (middle.astype(jnp.float32) + mixture).astype(jnp.bfloat16)


def on_device(
    tokens,
    prompt_lengths,
    cache_lengths,
    kv_cache,
    attn_routes,
    ffn_routes,
    attn_gain,
    ffn_gain,
    attn_mix,
    query_weight,
    kv_weight,
    out_weight,
    ffn_mix,
    in_weight,
    down_weight,
):
    batch = lax.axis_index("section")
    middle = attention_block(
        select_batch(tokens, batch),
        select_batch(prompt_lengths, batch),
        select_batch(cache_lengths, batch),
        select_batch(kv_cache, batch),
        select_batch(attn_routes, batch),
        attn_gain,
        attn_mix,
        query_weight,
        kv_weight,
        out_weight,
    )
    finished = expert_block(
        middle, select_batch(ffn_routes, batch), ffn_gain, ffn_mix, in_weight, down_weight
    )
    return finished[None]


def solution(mesh):
    return jax.shard_map(
        on_device,
        mesh=mesh,
        in_specs=(
            P(None, ("seq", "expert"), None),
            P(),
            P(),
            P(None, "seq", None, "expert"),
            P(None, "seq", None),
            P(None, ("seq", "expert"), None),
            P(),
            P(),
            P(),
            P(None, None, "expert"),
            P(None, None, "expert"),
            P(None, "expert", None),
            P(),
            P("expert", None, None, "seq"),
            P("expert", "seq", None),
        ),
        out_specs=P("section", ("seq", "expert"), None),
        check_vma=False,
    )
```

profile of v0, /device:TPU:1, one launch (start us, length us, event | category | flops | bytes accessed | tf_op | source)
XLA Modules:
  0.0 283.1 jit_solution(11401811092933586299)
XLA Ops:
  8.2 15.0 %all-gather = bf16[1,128,2048]{2,1,0:T(8,128)(2,1)S(1)} all-gather(bf16[1,16,2048]{2,1,0:T(8,128)(2,1)S(1)} %constant_dynamic-slice_fusion.5), channel_id=2, replica_groups=mesh['section'=2,'seq'=8,'expert'=8] {'expert'}, dimensions={1}, use_global_device_ids=true | all-gather | bytes 589824 | tf_op jit(solution)/shard_map/all_gather | solution.py:60
  23.3 3.4 %copy.115 = bf16[256,8,2,256]{3,1,2,0:T(8,128)(2,1)} copy(bf16[256,8,2,256]{3,2,1,0:T(2,128)(2,1)} %bitcast.189) | data formatting | bytes 4194304
  26.7 4.0 %copy.97 = bf16[512,2048]{1,0:T(8,128)(2,1)} copy(bf16[512,2048]{0,1:T(8,128)(2,1)} %bitcast.186) | data formatting | bytes 4194304 | tf_op jit(solution)/shard_map/dot_general | solution.py:76
  30.7 2.4 fusion.42
  41.0 1.8 constant_dynamic-slice_fusion.1
  42.8 1.8 copy.113
  48.3 2.4 gather_fusion.1
  51.0 5.2 %copy.114 = bf16[256,8,4,256]{3,1,2,0:T(8,128)(2,1)} copy(bf16[256,8,4,256]{3,2,1,0:T(4,128)(2,1)} %bitcast.187) | data formatting | bytes 8388608
  56.2 6.5 %copy.89 = bf16[1024,2048]{1,0:T(8,128)(2,1)} copy(bf16[1024,2048]{0,1:T(8,128)(2,1)} %bitcast.183) | data formatting | bytes 8388608 | tf_op jit(solution)/shard_map/dot_general | solution.py:69
  62.7 3.7 %fusion.44 = f32[128,4,2,128]{3,0,2,1:T(8,128)S(1)} fusion(bf16[4,2,128,2048]{3,2,1,0:T(8,128)(2,1)} %bitcast.182, bf16[1,128,2048]{2,1,0:T(8,128)(2,1)S(1)} %all-gather, f32[2048]{0:T(1024)S(1)} %copy-done.12, f32[128]{0:T(128)S(1)} %copy-done.23), kind=kOutput, calls=%fused_computation.52 | convolution fusion | flops 537919488 | bytes 5251584 | tf_op jit(solution)/shard_map/dot_general | solution.py:69
  66.9 1.9 gather_fusion.2
  73.4 2.0 subtract_convert_fusion
  75.7 5.5 %all-gather.5.cloned.1.call-done = bf16[1024,2,256]{0,2,1:T(8,128)(2,1)} async-done(((bf16[128,2,256]{0,2,1:T(8,128)(2,1)}), bf16[1024,2,256]{0,2,1:T(8,128)(2,1)}) %all-gather.5.cloned.1.call-update) | async-done | bytes 1048592 | tf_op jit(solution)/shard_map/all_gather | solution.py:114
  81.2 2.1 fusion.105
  83.3 2.0 fusion.15
  85.3 59.9 %all-gather.7.cloned.1.call-done = bf16[1,2048,2,256]{1,3,2,0:T(8,128)(2,1)} async-done(((bf16[1,256,2,256]{1,3,2,0:T(8,128)(2,1)}), bf16[1,2048,2,256]{1,3,2,0:T(8,128)(2,1)}) %all-gather.7.cloned.1.call-update) | async-done | bytes 2097168 | tf_op jit(solution)/shard_map/all_gather | solution.py:110
  154.0 3.7 %fusion.9 = bf16[128,2048]{1,0:T(8,128)(2,1)} fusion(bf16[4,256,2048]{2,1,0:T(8,128)(2,1)} %param.26, bf16[128,4,256]{2,1,0:T(4,128)(2,1)S(1)} %convolution_convert_fusion.2), kind=kOutput, calls=%fused_computation.16 | convolution fusion | flops 537133056 | bytes 4980736 | tf_op jit(solution)/shard_map/dot_general | solution.py:131
  158.7 30.2 %reduce-scatter.2.cloned.1.call-done = bf16[16,2048]{1,0:T(8,128)(2,1)} async-done(((bf16[128,2048]{1,0:T(8,128)(2,1)}), bf16[16,2048]{1,0:T(8,128)(2,1)}) %reduce-scatter.2.cloned.1.call-update) | async-done | bytes 65552 | tf_op jit(solution)/shard_map/reduce_scatter | solution.py:130
  190.4 38.1 %all_to_all.10 = bf16[64,8,2048]{2,1,0:T(8,128)(2,1)S(1)} all-to-all(bf16[64,8,2048]{2,1,0:T(8,128)(2,1)S(1)} %bitcast.185), channel_id=1, replica_groups=mesh['section'=2,'seq'=8,'expert'=8] {'seq','expert'}, dimensions={0} | all-to-all | bytes 4194304 | tf_op jit(solution)/shard_map/all_to_all | solution.py:167
  228.5 5.2 %fusion = f32[512,2,704]{0,2,1:T(8,128)S(1)} fusion(bf16[1,2048,2,704]{1,3,2,0:T(8,128)(2,1)} %param.28, bf16[64,8,2048]{2,1,0:T(8,128)(2,1)S(1)} %all_to_all.10), kind=kOutput, calls=%fused_computation.4 | convolution fusion | flops 2952790016 | bytes 10747904 | tf_op jit(solution)/shard_map/dot_general | solution.py:141
  233.7 3.3 %fusion.6 = bf16[64,8,2048]{2,1,0:T(8,128)(2,1)} fusion(bf16[1,704,2048]{2,1,0:T(8,128)(2,1)S(1)} %copy-done, f32[512,2,704]{0,2,1:T(8,128)S(1)} %fusion), kind=kOutput, calls=%fused_computation.14 | convolution fusion | flops 1479606272 | bytes 7864320 | tf_op jit(solution)/shard_map/dot_general | solution.py:170
  237.0 5.3 %all-to-all-start.1 = ((bf16[64,8,2048]{2,1,0:T(8,128)(2,1)}), bf16[64,8,2048]{2,1,0:T(8,128)(2,1)}, u32[]{:S(2)}, u32[]{:S(2)}) async-start(bf16[64,8,2048]{2,1,0:T(8,128)(2,1)} %fusion.6), calls=%async_computation.2 | async-start | bytes 4194304 | tf_op jit(solution)/shard_map/all_to_all | solution.py:172
  243.8 27.5 %all-to-all-done.1 = bf16[64,8,2048]{2,1,0:T(8,128)(2,1)} async-done(((bf16[64,8,2048]{2,1,0:T(8,128)(2,1)}), bf16[64,8,2048]{2,1,0:T(8,128)(2,1)}, u32[]{:S(2)}, u32[]{:S(2)}) %all-to-all-start.1) | async-done | bytes 2097184 | tf_op jit(solution)/shard_map/all_to_all | solution.py:172
  271.2 2.0 convert_reduce_fusion
  (144 shorter events, 34.7 us)
Async XLA Ops:
  6.5 227.2 %copy-start = (bf16[1,704,2048]{2,1,0:T(8,128)(2,1)S(1)}, bf16[1,704,2048]{2,1,0:T(8,128)(2,1)}, u32[]{:S(2)}) copy-start(bf16[1,704,2048]{2,1,0:T(8,128)(2,1)} %param.29) | copy-start | bytes 8650756
  6.5 74.7 %all-gather.5.cloned.1.call-start = ((), (), s32[]{:S(2)}) async-start(), calls=%async_computation.3 | async-start | bytes 1179648 | tf_op jit(solution)/shard_map/all_gather | solution.py:114
  23.3 7.4 %copy-start.22 = (f32[128]{0:T(128)}, f32[128]{0:T(128)S(1)}, u32[]{:S(2)}) copy-start(f32[128]{0:T(128)S(1)} %add_rsqrt_fusion.1) | copy-start | bytes 1540
  26.7 4.0 %copy-start.12 = (f32[2048]{0:T(1024)S(1)}, f32[2048]{0:T(1024)}, u32[]{:S(2)}) copy-start(f32[2048]{0:T(1024)} %param.21) | copy-start | bytes 24580
  30.7 3.1 %copy-start.17 = (s32[2,3]{1,0:T(2,128)S(1)}, s32[2,3]{1,0:T(2,128)}, u32[]{:S(2)}) copy-start(s32[2,3]{1,0:T(2,128)} %param.16) | copy-start | bytes 76
  30.7 3.1 %copy-start.24 = (s32[2,3]{1,0:T(2,128)S(1)}, s32[2,3]{1,0:T(2,128)}, u32[]{:S(2)}) copy-start(s32[2,3]{1,0:T(2,128)} %param.17) | copy-start | bytes 76
  33.1 14.6 %copy-start.14 = (s32[2,128,2]{1,2,0:T(2,128)S(1)}, s32[2,128,2]{1,2,0:T(2,128)}, u32[]{:S(2)}) copy-start(s32[2,128,2]{1,2,0:T(2,128)} %param.19) | copy-start | bytes 6148
  39.4 8.5 %copy-start.23 = (f32[128]{0:T(128)S(1)}, f32[128]{0:T(128)}, u32[]{:S(2)}) copy-start(f32[128]{0:T(128)} %copy-done.22) | copy-start | bytes 1540
  39.4 8.6 %copy-start.26 = (bf16[2048,4]{0,1:T(4,128)(2,1)S(1)}, bf16[2048,4]{0,1:T(4,128)(2,1)}, u32[]{:S(2)}) copy-start(bf16[2048,4]{0,1:T(4,128)(2,1)} %param.23) | copy-start | bytes 49156
  41.0 104.3 %all-gather.7.cloned.1.call-start = ((), (), s32[]{:S(2)}) async-start(), calls=%async_computation.5 | async-start | bytes 2359296 | tf_op jit(solution)/shard_map/all_gather | solution.py:110
  44.7 144.2 %reduce-scatter.2.cloned.1.call-start = ((), (), s32[]{:S(2)}) async-start(), calls=%async_computation.4 | async-start | bytes 589824 | tf_op jit(solution)/shard_map/reduce_scatter | solution.py:130
  62.7 6.3 %copy-start.19 = (s32[128]{0:T(128)S(1)}, s32[128]{0:T(128)}, u32[]{:S(2)}) copy-start(s32[128]{0:T(128)} %copy-done.18) | copy-start | bytes 1540
  62.7 6.6 %copy-start.21 = (s32[3,1]{0,1:T(1,128)S(1)}, s32[3,1]{0,1:T(1,128)}, u32[]{:S(2)}) copy-start(s32[3,1]{0,1:T(1,128)} %get-tuple-element.33) | copy-start | bytes 40
  62.7 8.2 %copy-start.16 = (s32[3,1]{0,1:T(1,128)S(1)}, s32[3,1]{0,1:T(1,128)}, u32[]{:S(2)}) copy-start(s32[3,1]{0,1:T(1,128)} %copy-done.15) | copy-start | bytes 40
  81.2 2.1 copy-start.2
  81.2 2.1 copy-start.4
  145.3 1.8 copy-start.5
  148.3 1.6 copy-start.1
  148.3 1.6 copy-start.3
  153.9 3.8 %copy-start.20 = (s32[2,16,2]{1,2,0:T(2,128)S(1)}, s32[2,16,2]{1,2,0:T(2,128)}, u32[]{:S(2)}) copy-start(s32[2,16,2]{1,2,0:T(2,128)} %param.20) | copy-start | bytes 772
  153.9 34.9 %copy-start.9 = (bf16[2,16,2048]{2,1,0:T(8,128)(2,1)S(1)}, bf16[2,16,2048]{2,1,0:T(8,128)(2,1)}, u32[]{:S(2)}) copy-start(bf16[2,16,2048]{2,1,0:T(8,128)(2,1)} %param.15) | copy-start | bytes 393220
  153.9 35.9 %copy-start.13 = (f32[2048]{0:T(1024)S(1)}, f32[2048]{0:T(1024)}, u32[]{:S(2)}) copy-start(f32[2048]{0:T(1024)} %param.22) | copy-start | bytes 24580
  237.0 5.7 %copy-start.25 = (bf16[2048,8]{0,1:T(8,128)(2,1)S(1)}, bf16[2048,8]{0,1:T(8,128)(2,1)}, u32[]{:S(2)}) copy-start(bf16[2048,8]{0,1:T(8,128)(2,1)} %param.27) | copy-start | bytes 98308
  237.0 34.2 %all-to-all-start.1 = ((bf16[64,8,2048]{2,1,0:T(8,128)(2,1)}), bf16[64,8,2048]{2,1,0:T(8,128)(2,1)}, u32[]{:S(2)}, u32[]{:S(2)}) async-start(bf16[64,8,2048]{2,1,0:T(8,128)(2,1)} %fusion.6), calls=%async_computation.2 | async-start | bytes 4194304 | tf_op jit(solution)/shard_map/all_to_all | solution.py:172
  (7 other events, 6.8 us)
Sparse Core Ops, SparseCore 0:
  41.1 40.0 all-gather.4
  82.8 62.4 all-gather.6
  157.8 31.0 reduce-scatter.1
where the time goes:
time: 284 us; the launch traced here: 283 us
  waiting for transfers between devices  123 us (43%)
  blocking collectives  53 us (19%)
  local copies, waits for them, and re-layouts  44.3 us (16%)
  matrix products  25.3 us (9%)
  other arithmetic  18.4 us (6%)
  between operations  13.6 us (5%)
  starting transfers between devices  5.34 us (2%)
    all_gather x1, waiting for transfers between devices, attention_block(): piece = lax.all_gather(cache_rows, 'seq', axis=0, tiled=True)  59.9 us
    all_to_all x1, blocking collectives, expert_block(): lax.all_to_all(copies, ('seq', 'expert'), split_axis=0, concat_axis=0, ti...  38.1 us
    reduce_scatter x1, waiting for transfers between devices, attention_block(): lax.psum_scatter(jnp.dot(spread, out_flat, preferred_element_type=jnp.flo...  30.2 us
    all_to_all x1, waiting for transfers between devices, expert_block(): lax.all_to_all(partial_value, ('seq', 'expert'), split_axis=0, concat_axi...  27.5 us
    all_gather x1, blocking collectives, attention_block(): gathered = lax.all_gather(own_rows, 'expert', axis=0, tiled=True)  15 us
    unnamed x57, local copies, waits for them, and re-layouts  11.2 us
    dot_general x2, local copies, waits for them, and re-layouts, attention_block(): jnp.dot(normed, query_weight.reshape(query_weight.shape[0], -1), preferre...  6.91 us
  transfers between devices with their start and end apart: 4, of which 4 were waited for; matrix products, arithmetic and copies ran while one was open for 14% of the time, Pallas kernels for 0%

commit v1 on v0

--- a/solution.py
+++ b/solution.py
@@ -57,7 +57,9 @@
 def attention_block(
     own_rows, lengths, cached, cache_rows, routes, gain, mixing, query_weight, kv_weight, out_weight
 ):
-    gathered = lax.all_gather(own_rows, "expert", axis=0, tiled=True)
+    gathered = jnp.concatenate(
+        lax.all_to_all(jnp.stack([own_rows] * lax.axis_size("expert")), "expert", 0, 0), axis=0
+    )
     count = gathered.shape[0]
     normed = rms_scale(gathered, gain)
     row_index = lax.axis_index("seq") * count + jnp.arange(count, dtype=jnp.int32)

time: 284 us -> 273 us (0.961)
  blocking collectives: 53 us -> 37.9 us
  waiting for transfers between devices: 123 us -> 117 us
  starting transfers between devices: 5.34 us -> 11.3 us
  local copies, waits for them, and re-layouts: 44.3 us -> 49.7 us
    all_gather x1 -> x0, blocking collectives: 15 us -> none  [attention_block(): gathered = lax.all_gather(own_rows, 'expert', axis=0, tiled=True)]
    all_to_all x0 -> x1, starting transfers between devices: none -> 5.97 us  [attention_block(): lax.all_to_all(jnp.stack([own_rows] * lax.axis_size('expert')), 'expert',...]
    all_gather x1, waiting for transfers between devices: 5.47 us -> 0.02 us  [attention_block(): piece = lax.all_gather(fresh, 'seq', axis=0, tiled=True)]
    unnamed x57 -> x41, local copies, waits for them, and re-layouts: 11.2 us -> 11.9 us
  transfers between devices with their start and end apart: 4 -> 5, of which waited for: 4 -> 3; matrix products, arithmetic and copies ran while one was open for 14% -> 21% of each run, Pallas kernels for 0% -> 0%
where the time goes in v1:
time: 273 us; the launch traced here: 272 us
  waiting for transfers between devices  117 us (43%)
  local copies, waits for them, and re-layouts  49.7 us (18%)
  blocking collectives  37.9 us (14%)
  matrix products  25.9 us (9%)
  other arithmetic  16.3 us (6%)
  between operations  13.6 us (5%)
  starting transfers between devices  11.3 us (4%)
    all_gather x1, waiting for transfers between devices, attention_block(): piece = lax.all_gather(cache_rows, 'seq', axis=0, tiled=True)  59.3 us
    all_to_all x1, blocking collectives, expert_block(): lax.all_to_all(copies, ('seq', 'expert'), split_axis=0, concat_axis=0, ti...  37.9 us
    reduce_scatter x1, waiting for transfers between devices, attention_block(): lax.psum_scatter(jnp.dot(spread, out_flat, preferred_element_type=jnp.flo...  30.4 us
    all_to_all x1, waiting for transfers between devices, expert_block(): lax.all_to_all(partial_value, ('seq', 'expert'), split_axis=0, concat_axi...  27.5 us
    unnamed x41, local copies, waits for them, and re-layouts  11.9 us
    dot_general x2, local copies, waits for them, and re-layouts, attention_block(): jnp.dot(normed, query_weight.reshape(query_weight.shape[0], -1), preferre...  7.73 us
    all_to_all x1, starting transfers between devices, attention_block(): lax.all_to_all(jnp.stack([own_rows] * lax.axis_size('expert')), 'expert',...  5.97 us
    gather x10, local copies, waits for them, and re-layouts, route_gates(): chosen = jnp.take_along_axis(logits, routes, axis=1)  5.5 us
  transfers between devices with their start and end apart: 5, of which 3 were waited for; matrix products, arithmetic and copies ran while one was open for 21% of the time, Pallas kernels for 0%

profile of v1, /device:TPU:1, one launch (start us, length us, event | category | flops | bytes accessed | tf_op | source)
XLA Modules:
  0.0 272.0 jit_solution(5673191680287351649)
XLA Ops:
  8.4 6.0 %all-to-all-start = ((bf16[8,16,2048]{2,1,0:T(8,128)(2,1)}), bf16[8,16,2048]{2,1,0:T(8,128)(2,1)S(1)}, u32[]{:S(2)}, u32[]{:S(2)}) async-start(bf16[8,16,2048]{2,1,0:T(8,128)(2,1)} %stack.6), calls=%async_computation | async-start | bytes 1048576 | tf_op jit(solution)/shard_map/all_to_all | solution.py:61
  17.1 3.3 %copy.115 = bf16[256,8,2,256]{3,1,2,0:T(8,128)(2,1)} copy(bf16[256,8,2,256]{3,2,1,0:T(2,128)(2,1)} %bitcast.188) | data formatting | bytes 4194304
  20.5 4.0 %copy.97 = bf16[512,2048]{1,0:T(8,128)(2,1)} copy(bf16[512,2048]{0,1:T(8,128)(2,1)} %bitcast.183) | data formatting | bytes 4194304 | tf_op jit(solution)/shard_map/dot_general | solution.py:78
  25.9 2.3 fusion.97
  29.0 1.8 constant_dynamic-slice_fusion.1
  30.8 1.8 copy.113
  34.5 5.2 %copy.114 = bf16[256,8,4,256]{3,1,2,0:T(8,128)(2,1)} copy(bf16[256,8,4,256]{3,2,1,0:T(4,128)(2,1)} %bitcast.186) | data formatting | bytes 8388608
  39.7 6.5 %copy.89 = bf16[1024,2048]{1,0:T(8,128)(2,1)} copy(bf16[1024,2048]{0,1:T(8,128)(2,1)} %bitcast.179) | data formatting | bytes 8388608 | tf_op jit(solution)/shard_map/dot_general | solution.py:71
  52.4 1.8 broadcast_compare_fusion
  55.5 2.6 gather_fusion.1
  60.5 3.7 %fusion.96 = f32[128,4,2,128]{3,0,2,1:T(8,128)S(1)} fusion(bf16[128,2048,1,1]{1,0,3,2:T(8,128)(2,1)S(1)} %bitcast.185, bf16[4,2,128,2048]{3,2,1,0:T(8,128)(2,1)} %bitcast.178), kind=kOutput, calls=%fused_computation.167 | convolution fusion | flops 536870912 | bytes 5242880 | tf_op jit(solution)/shard_map/dot_general | solution.py:71
  65.5 2.3 gather_fusion.2
  70.7 2.1 fusion.94
  72.8 2.0 fusion.15
  74.8 59.3 %all-gather.6.cloned.1.call-done = bf16[1,2048,2,256]{1,3,2,0:T(8,128)(2,1)} async-done(((bf16[1,256,2,256]{1,3,2,0:T(8,128)(2,1)}), bf16[1,2048,2,256]{1,3,2,0:T(8,128)(2,1)}) %all-gather.6.cloned.1.call-update) | async-done | bytes 2097168 | tf_op jit(solution)/shard_map/all_gather | solution.py:112
  134.1 1.8 fusion.93
  142.9 3.7 %fusion.9 = bf16[128,2048]{1,0:T(8,128)(2,1)} fusion(bf16[4,256,2048]{2,1,0:T(8,128)(2,1)} %param.26, bf16[128,4,256]{2,1,0:T(4,128)(2,1)S(1)} %convolution_convert_fusion.2), kind=kOutput, calls=%fused_computation.16 | convolution fusion | flops 537133056 | bytes 4980736 | tf_op jit(solution)/shard_map/dot_general | solution.py:133
  147.4 30.4 %reduce-scatter.2.cloned.1.call-done = bf16[16,2048]{1,0:T(8,128)(2,1)} async-done(((bf16[128,2048]{1,0:T(8,128)(2,1)}), bf16[16,2048]{1,0:T(8,128)(2,1)}) %reduce-scatter.2.cloned.1.call-update) | async-done | bytes 65552 | tf_op jit(solution)/shard_map/reduce_scatter | solution.py:132
  179.4 37.9 %all_to_all.15 = bf16[64,8,2048]{2,1,0:T(8,128)(2,1)S(1)} all-to-all(bf16[64,8,2048]{2,1,0:T(8,128)(2,1)S(1)} %bitcast.182), channel_id=1, replica_groups=mesh['section'=2,'seq'=8,'expert'=8] {'seq','expert'}, dimensions={0} | all-to-all | bytes 4194304 | tf_op jit(solution)/shard_map/all_to_all | solution.py:169
  217.3 5.2 %fusion = f32[512,2,704]{0,2,1:T(8,128)S(1)} fusion(bf16[1,2048,2,704]{1,3,2,0:T(8,128)(2,1)} %param.28, bf16[64,8,2048]{2,1,0:T(8,128)(2,1)S(1)} %all_to_all.15), kind=kOutput, calls=%fused_computation.4 | convolution fusion | flops 2952790016 | bytes 10747904 | tf_op jit(solution)/shard_map/dot_general | solution.py:143
  222.6 3.3 %fusion.6 = bf16[64,8,2048]{2,1,0:T(8,128)(2,1)} fusion(bf16[1,704,2048]{2,1,0:T(8,128)(2,1)S(1)} %copy-done, f32[512,2,704]{0,2,1:T(8,128)S(1)} %fusion), kind=kOutput, calls=%fused_computation.14 | convolution fusion | flops 1479606272 | bytes 7864320 | tf_op jit(solution)/shard_map/dot_general | solution.py:172
  225.9 5.3 %all-to-all-start.2 = ((bf16[64,8,2048]{2,1,0:T(8,128)(2,1)}), bf16[64,8,2048]{2,1,0:T(8,128)(2,1)}, u32[]{:S(2)}, u32[]{:S(2)}) async-start(bf16[64,8,2048]{2,1,0:T(8,128)(2,1)} %fusion.6), calls=%async_computation.3 | async-start | bytes 4194304 | tf_op jit(solution)/shard_map/all_to_all | solution.py:174
  232.6 27.5 %all-to-all-done.2 = bf16[64,8,2048]{2,1,0:T(8,128)(2,1)} async-done(((bf16[64,8,2048]{2,1,0:T(8,128)(2,1)}), bf16[64,8,2048]{2,1,0:T(8,128)(2,1)}, u32[]{:S(2)}, u32[]{:S(2)}) %all-to-all-start.2) | async-done | bytes 2097184 | tf_op jit(solution)/shard_map/all_to_all | solution.py:174
  260.1 2.0 convert_reduce_fusion
  (133 shorter events, 36.4 us)
Async XLA Ops:
  6.5 216.0 %copy-start = (bf16[1,704,2048]{2,1,0:T(8,128)(2,1)S(1)}, bf16[1,704,2048]{2,1,0:T(8,128)(2,1)}, u32[]{:S(2)}) copy-start(bf16[1,704,2048]{2,1,0:T(8,128)(2,1)} %param.29) | copy-start | bytes 8650756
  8.4 16.3 %all-to-all-start = ((bf16[8,16,2048]{2,1,0:T(8,128)(2,1)}), bf16[8,16,2048]{2,1,0:T(8,128)(2,1)S(1)}, u32[]{:S(2)}, u32[]{:S(2)}) async-start(bf16[8,16,2048]{2,1,0:T(8,128)(2,1)} %stack.6), calls=%async_computation | async-start | bytes 1048576 | tf_op jit(solution)/shard_map/all_to_all | solution.py:61
  14.3 56.4 %all-gather.4.cloned.1.call-start = ((), (), s32[]{:S(2)}) async-start(), calls=%async_computation.4 | async-start | bytes 1179648 | tf_op jit(solution)/shard_map/all_gather | solution.py:116
  15.7 4.7 %copy-start.15 = (s32[3,1]{0,1:T(1,128)}, s32[3,1]{0,1:T(1,128)S(1)}, u32[]{:S(2)}) copy-start(s32[3,1]{0,1:T(1,128)S(1)} %reduce-window.13) | copy-start | bytes 40
  16.4 0.7 copy-start.16
  16.5 0.5 copy-start.13
  20.5 4.4 %copy-start.10 = (f32[2048]{0:T(1024)S(1)}, f32[2048]{0:T(1024)}, u32[]{:S(2)}) copy-start(f32[2048]{0:T(1024)} %param.21) | copy-start | bytes 24580
  25.1 0.8 copy-start.2
  29.0 105.1 %all-gather.6.cloned.1.call-start = ((), (), s32[]{:S(2)}) async-start(), calls=%async_computation.6 | async-start | bytes 2359296 | tf_op jit(solution)/shard_map/all_gather | solution.py:112
  32.7 145.2 %reduce-scatter.2.cloned.1.call-start = ((), (), s32[]{:S(2)}) async-start(), calls=%async_computation.5 | async-start | bytes 589824 | tf_op jit(solution)/shard_map/reduce_scatter | solution.py:132
  55.5 4.3 %copy-start.14 = (s32[2,128,2]{1,2,0:T(2,128)S(1)}, s32[2,128,2]{1,2,0:T(2,128)}, u32[]{:S(2)}) copy-start(s32[2,128,2]{1,2,0:T(2,128)} %param.19) | copy-start | bytes 6148
  55.5 5.0 %copy-start.3 = (bf16[8,16,2048]{2,1,0:T(8,128)(2,1)S(1)}, bf16[8,16,2048]{2,1,0:T(8,128)(2,1)}, u32[]{:S(2)}) copy-start(bf16[8,16,2048]{2,1,0:T(8,128)(2,1)} %copy-done.2) | copy-start | bytes 1572868
  64.2 6.0 %copy-start.7 = (f32[128,64]{1,0:T(8,128)S(1)}, f32[128,64]{1,0:T(8,128)}, u32[]{:S(2)}) copy-start(f32[128,64]{1,0:T(8,128)} %copy.93) | copy-start | bytes 98308
  65.5 7.4 %copy-start.5 = (pred[256,1024]{1,0:T(8,128)(4,1)S(1)}, pred[256,1024]{1,0:T(8,128)(4,1)}, u32[]{:S(2)}) copy-start(pred[256,1024]{1,0:T(8,128)(4,1)} %fusion.37) | copy-start | bytes 786436
  134.1 1.8 copy-start.4
  137.2 1.6 copy-start.1
  139.6 1.5 copy-start.6
  141.1 1.1 copy-start.9
  141.1 1.1 copy-start.11
  142.9 3.8 %copy-start.17 = (s32[2,16,2]{1,2,0:T(2,128)S(1)}, s32[2,16,2]{1,2,0:T(2,128)}, u32[]{:S(2)}) copy-start(s32[2,16,2]{1,2,0:T(2,128)} %param.20) | copy-start | bytes 772
  142.9 35.0 %copy-start.8 = (bf16[2,16,2048]{2,1,0:T(8,128)(2,1)S(1)}, bf16[2,16,2048]{2,1,0:T(8,128)(2,1)}, u32[]{:S(2)}) copy-start(bf16[2,16,2048]{2,1,0:T(8,128)(2,1)} %param.15) | copy-start | bytes 393220
  142.9 36.0 %copy-start.12 = (f32[2048]{0:T(1024)S(1)}, f32[2048]{0:T(1024)}, u32[]{:S(2)}) copy-start(f32[2048]{0:T(1024)} %param.22) | copy-start | bytes 24580
  225.9 5.7 %copy-start.18 = (bf16[2048,8]{0,1:T(8,128)(2,1)S(1)}, bf16[2048,8]{0,1:T(8,128)(2,1)}, u32[]{:S(2)}) copy-start(bf16[2048,8]{0,1:T(8,128)(2,1)} %param.27) | copy-start | bytes 98308
  225.9 34.2 %all-to-all-start.2 = ((bf16[64,8,2048]{2,1,0:T(8,128)(2,1)}), bf16[64,8,2048]{2,1,0:T(8,128)(2,1)}, u32[]{:S(2)}, u32[]{:S(2)}) async-start(bf16[64,8,2048]{2,1,0:T(8,128)(2,1)} %fusion.6), calls=%async_computation.3 | async-start | bytes 4194304 | tf_op jit(solution)/shard_map/all_to_all | solution.py:174
Sparse Core Ops, SparseCore 0:
  29.1 41.0 all-gather.3
  71.7 62.3 all-gather.5
  146.8 31.0 reduce-scatter.1
